TPU v7x, 32 devices: a whole 2x2x4 slice. The times are simulated.
32 devices in a mesh: gx: 8 (over z, y), gy: 4 (over x, core).
Axes of the slice: x: 2, y: 2, z: 4, core: 2. Of those that a mesh axis runs over, the one named last changes fastest.
Arguments:
- fuel: float32 [16, 768, 384], P('gx', 'gy'), may hold values from -41 to 41, as said below
- oxidizer: float32 [16, 768, 384], P('gx', 'gy'), may hold values from -41 to 41, as said below
- kappa: float32 [16, 768, 384], P('gx', 'gy'), may hold values from 0.05 to 0.5
- rate: float32 [16, 768, 384], P('gx', 'gy'), may hold values from 0.5 to 5
Outputs:
- fuel_next: float32 [16, 768, 384], P('gx', 'gy')
- oxid_next: float32 [16, 768, 384], P('gx', 'gy')
- r_factor: float32 [384, 384], replicated
Inputs may be any that keep to these rules, and one draw needn't show every extreme that they name: `fuel`: A real-valued field. `oxidizer`: A real-valued field.
All inputs are finite; a program needn't handle non-finite values.
Results may differ from a plain program's by a relative error of at most 0.000067.
Values sent between devices are 32-bit elements; how exact they have to be, the bound alone decides.
A program may use at most 64 MiB of HBM per device.

v0:
```python
import jax
import jax.numpy as jnp
from jax import lax
from jax.sharding import PartitionSpec as P


def extended(cells, sides, width):
    for axis, dim in sides:
        count = lax.axis_size(axis)
        ends = count - 1
        head = lax.slice_in_dim(cells, 0, width, axis=dim)
        tail = lax.slice_in_dim(cells, cells.shape[dim] - width, cells.shape[dim], axis=dim)
        cells = jnp.concatenate(
            [
                lax.ppermute(tail, axis, [(i, (i + 1) % count) for i in range(ends)]),
                cells,
                lax.ppermute(head, axis, [((i + 1) % count, i) for i in range(ends)]),
            ],
            axis=dim,
        )
    return cells


def diffuse_local(padded, kpad):
    planes = padded.shape[0] - 2
    width = padded.shape[1] - 2
    total = jnp.zeros((planes, width, padded.shape[2] - 2), jnp.float32)
    center = padded[1:-1, 1:-1, 1:-1]
    kcenter = kpad[1:-1, 1:-1, 1:-1]
    sizes = (planes, width, padded.shape[2] - 2)
    for axis in range(3):
        for offset in (0, 2):
            index = [slice(1, -1)] * 3
            index[axis] = slice(offset, offset + sizes[axis])
            index = tuple(index)
            total = total + 0.5 * (kcenter + kpad[index]) * (padded[index] - center)
    return total


def local_gram(first, second):
    flat_a = first.reshape(-1, first.shape[2])
    flat_b = second.reshape(-1, second.shape[2])
    dims = (((0,), (0,)), ((), ()))
    gram = lax.dot_general(flat_a, flat_a, dims, precision=lax.Precision.HIGHEST)
    return gram + lax.dot_general(flat_b, flat_b, dims, precision=lax.Precision.HIGHEST)


def shards(fuel, oxidizer, kappa, rate):
    stacked = jnp.stack([fuel, oxidizer, kappa])
    widened = extended(stacked, (("gx", 1), ("gy", 2)), 1)
    widened = jnp.pad(widened, ((0, 0), (0, 0), (0, 0), (1, 1)))
    prod = fuel * oxidizer
    react = rate * prod / jnp.sqrt(1.0 + prod * prod)
    fuel_next = fuel + 0.15 * (diffuse_local(widened[0], widened[2]) - react)
    oxid_next = oxidizer + 0.15 * (diffuse_local(widened[1], widened[2]) + react)
    rows = 2 * fuel.shape[0] * fuel.shape[1] * lax.axis_size("gx") * lax.axis_size("gy")
    gram = local_gram(fuel_next, oxid_next) / rows
    total = lax.psum(gram, ("gx", "gy"))
    factor = jnp.linalg.cholesky(total).T
    return (fuel_next, oxid_next, factor)


def solution(mesh):
    in_specs = (P("gx", "gy", None), P("gx", "gy", None), P("gx", "gy", None), P("gx", "gy", None))
    out_specs = (P("gx", "gy", None), P("gx", "gy", None), P())
    return jax.shard_map(shards, mesh=mesh, in_specs=in_specs, out_specs=out_specs, check_vma=False)
```

profile of v0, /device:TPU:0, one launch (start us, length us, event | category | flops | bytes accessed | tf_op | source)
XLA Modules:
  0.0 272.9 jit_solution(1757577690455986732)
XLA Ops:
  7.2 0.0 copy-start.1
  7.2 0.0 copy-start
  7.2 0.0 copy-start.2
  7.2 0.0 all-reduce.4.cloned.1.call-start
  7.2 1.7 pad_maximum_fusion
  8.9 0.1 fusion.45
  9.0 5.0 %collective-permute-start = (f32[3,1,192,384]{3,2,1,0:T(8,128)S(1)}, f32[3,1,192,384]{3,2,1,0:T(8,128)S(1)}, u32[]{:S(2)}, u32[]{:S(2)}) collective-permute-start(f32[3,1,192,384]{3,2,1,0:T(8,128)S(1)} %get-tuple-element.11), channel_id=1, source_target_pairs={{0,4},{4,8},{8,12},{12,16},{16,20},{20,24},{24,28},{1,5},{5,9},{9,... | collective-permute-start | bytes 2654216 | tf_op jit(solution)/shard_map/ppermute | solution.py:15
  14.0 1.3 collective-permute-start.1
  15.3 36.5 %collective-permute-done = f32[3,1,192,384]{3,2,1,0:T(8,128)S(1)} collective-permute-done((f32[3,1,192,384]{3,2,1,0:T(8,128)S(1)}, f32[3,1,192,384]{3,2,1,0:T(8,128)S(1)}, u32[]{:S(2)}, u32[]{:S(2)}) %collective-permute-start) | collective-permute-done | bytes 884768 | tf_op jit(solution)/shard_map/ppermute | solution.py:15
  51.8 0.0 collective-permute-done.1
  51.8 0.0 copy-done.1
  51.8 0.0 copy-done
  51.8 0.0 copy-done.2
  51.8 1.3 collective-permute-start.2
  53.1 1.3 collective-permute-start.3
  54.4 0.0 collective-permute-done.2
  54.4 3.5 %collective-permute-done.3 = f32[3,4,1,384]{3,2,1,0:T(1,128)S(1)} collective-permute-done((f32[3,4,1,384]{3,2,1,0:T(1,128)S(1)}, f32[3,4,1,384]{3,2,1,0:T(1,128)S(1)}, u32[]{:S(2)}, u32[]{:S(2)}) %collective-permute-start.3) | collective-permute-done | bytes 18464 | tf_op jit(solution)/shard_map/ppermute | solution.py:17
  57.9 4.8 %select_maximum_fusion = f32[3,4,194,386]{3,2,1,0:T(8,128)S(1)} fusion(f32[3,4,1,384]{3,2,1,0:T(1,128)S(1)} %collective-permute-done.3, f32[3,4,1,384]{3,2,1,0:T(1,128)S(1)} %collective-permute-done.2, f32[3,1,192,384]{3,2,1,0:T(8,128)S(1)} %collective-permute-done.1, f32[3,1,192,384]{3,2,1,0:T(8,128)S(1)} %collective-permute-done, ...), kind=kLoop, calls=%fused_computation.2 | loop fusion | flops 14377728 | bytes 7170240 | tf_op jit(solution)/shard_map/concatenate | solution.py:13
  62.7 0.0 copy-start.5
  62.7 0.5 slice_bitcast_fusion
  63.3 0.5 copy-done.5
  63.8 2.0 fusion.7
  65.8 0.0 copy-start.3
  65.8 2.0 fusion.21
  67.9 0.0 copy-done.3
  67.9 0.0 copy-start.4
  67.9 1.4 convolution_bitcast_fusion
  69.3 2.2 fusion.2
  71.5 0.0 all-reduce.4.cloned.1.call-update
  71.5 131.7 %all-reduce.4.cloned.1.call-done = f32[384,384]{0,1:T(8,128)} async-done(((f32[384,384]{0,1:T(8,128)}), f32[384,384]{0,1:T(8,128)}) %all-reduce.4.cloned.1.call-update) | async-done | bytes 589840 | tf_op jit(solution)/shard_map/psum | solution.py:58
  203.2 1.3 copy.9
  204.5 1.1 fusion.37
  205.6 11.7 %cholesky.77 = f32[128,128]{1,0:T(8,128)S(1)} custom-call(f32[128,128]{1,0:T(8,128)S(1)} %cholesky.192), custom_call_target="Cholesky" | custom-call | tf_op jit(solution)/shard_map/jit(cholesky)/cholesky | solution.py:59
  217.4 10.0 %custom-call.19 = f32[1,128,128]{1,2,0:T(8,128)S(1)} custom-call(f32[1,128,128]{2,1,0:T(8,128)S(1)} %get-tuple-element.19), custom_call_target="InvertDiagBlocksLowerTriangular" | custom-call | tf_op jit(solution)/shard_map/jit(cholesky)/cholesky | solution.py:59
  227.4 0.3 constant_dynamic-update-slice_fusion.1
  227.7 0.3 convolution_subtract_fusion
  228.0 11.7 %cholesky.162 = f32[128,128]{1,0:T(8,128)S(1)} custom-call(f32[128,128]{1,0:T(8,128)S(1)} %cholesky.196), custom_call_target="Cholesky" | custom-call | tf_op jit(solution)/shard_map/jit(cholesky)/cholesky | solution.py:59
  239.7 0.0 copy-done.4
  239.7 9.8 %custom-call.20 = f32[1,128,128]{1,2,0:T(8,128)S(1)} custom-call(f32[1,128,128]{2,1,0:T(8,128)S(1)} %get-tuple-element.16), custom_call_target="InvertDiagBlocksLowerTriangular" | custom-call | tf_op jit(solution)/shard_map/jit(cholesky)/cholesky | solution.py:59
  249.5 0.2 convolution_dynamic-update-slice_fusion
  249.7 0.3 convolution_subtract_fusion.1
  250.0 11.7 %cholesky.181 = f32[128,128]{1,0:T(8,128)S(1)} custom-call(f32[128,128]{1,0:T(8,128)S(1)} %convolution_subtract_fusion.1), custom_call_target="Cholesky" | custom-call | tf_op jit(solution)/shard_map/jit(cholesky)/cholesky | solution.py:59
  261.8 0.6 compare_reduce_fusion
  262.4 0.7 compare_reduce_fusion.1
  265.0 1.1 copy.10
  (8 shorter events, 0.2 us)
Async XLA Ops:
  7.2 44.6 %copy-start.1 = (f32[2,192,384]{2,1,0:T(8,128)S(1)}, f32[2,192,384]{2,1,0:T(8,128)}, u32[]{:S(2)}) copy-start(f32[2,192,384]{2,1,0:T(8,128)} %param.5) | copy-start | bytes 1769476
  7.2 44.6 %copy-start = (f32[2,192,384]{2,1,0:T(8,128)S(1)}, f32[2,192,384]{2,1,0:T(8,128)}, u32[]{:S(2)}) copy-start(f32[2,192,384]{2,1,0:T(8,128)} %param.4) | copy-start | bytes 1769476
  7.2 44.6 %copy-start.2 = (f32[2,192,384]{2,1,0:T(8,128)S(1)}, f32[2,192,384]{2,1,0:T(8,128)}, u32[]{:S(2)}) copy-start(f32[2,192,384]{2,1,0:T(8,128)} %param.6) | copy-start | bytes 1769476
  7.2 196.0 %all-reduce.4.cloned.1.call-start = ((), (), s32[]{:S(2)}) async-start(), calls=%async_computation | async-start | bytes 1179648 | tf_op jit(solution)/shard_map/psum | solution.py:58
  9.0 42.8 %collective-permute-start = (f32[3,1,192,384]{3,2,1,0:T(8,128)S(1)}, f32[3,1,192,384]{3,2,1,0:T(8,128)S(1)}, u32[]{:S(2)}, u32[]{:S(2)}) collective-permute-start(f32[3,1,192,384]{3,2,1,0:T(8,128)S(1)} %get-tuple-element.11), channel_id=1, source_target_pairs={{0,4},{4,8},{8,12},{12,16},{16,20},{20,24},{24,28},{1,5},{5,9},{9,... | collective-permute-start | bytes 2654216 | tf_op jit(solution)/shard_map/ppermute | solution.py:15
  14.0 37.8 %collective-permute-start.1 = (f32[3,1,192,384]{3,2,1,0:T(8,128)S(1)}, f32[3,1,192,384]{3,2,1,0:T(8,128)S(1)}, u32[]{:S(2)}, u32[]{:S(2)}) collective-permute-start(f32[3,1,192,384]{3,2,1,0:T(8,128)S(1)} %get-tuple-element.12), channel_id=1, source_target_pairs={{4,0},{8,4},{12,8},{16,12},{20,16},{24,20},{28,24},{5,1},{9,5},{13... | collective-permute-start | bytes 2654216 | tf_op jit(solution)/shard_map/ppermute | solution.py:17
  51.8 2.6 collective-permute-start.2
  53.1 4.8 %collective-permute-start.3 = (f32[3,4,1,384]{3,2,1,0:T(1,128)S(1)}, f32[3,4,1,384]{3,2,1,0:T(1,128)S(1)}, u32[]{:S(2)}, u32[]{:S(2)}) collective-permute-start(f32[3,4,1,384]{3,2,1,0:T(1,128)S(1)} %get-tuple-element.10), channel_id=1, source_target_pairs={{1,0},{2,1},{3,2},{5,4},{6,5},{7,6},{9,8},{10,9},{11,10},{13,12},{... | collective-permute-start | bytes 55304 | tf_op jit(solution)/shard_map/ppermute | solution.py:17
  62.7 1.1 copy-start.5
  65.8 2.1 copy-start.3
  67.9 171.8 %copy-start.4 = (f32[2,192,384]{2,1,0:T(8,128)}, f32[2,192,384]{2,1,0:T(8,128)S(1)}, u32[]{:S(2)}) copy-start(f32[2,192,384]{2,1,0:T(8,128)S(1)} %fusion.21) | copy-start | bytes 1769476
Sparse Core Ops, SparseCore 0:
  71.6 131.5 all-reduce.3
where the time goes:
time: 273 us
  waiting for transfers between devices  172 us (63%)
  other arithmetic  68 us (25%)
  between operations  16.1 us (6%)
  starting transfers between devices  8.87 us (3%)
  matrix products  4.56 us (2%)
  local copies, waits for them, and re-layouts  3.59 us (1%)
    psum x1, waiting for transfers between devices, shards(): total = lax.psum(gram, ('gx', 'gy'))  132 us
    another operation x10, other arithmetic, shards(): factor = jnp.linalg.cholesky(total).T  56.3 us
    ppermute x2, waiting for transfers between devices, extended(): lax.ppermute(tail, axis, [(i, (i + 1) % count) for i in range(ends)])  36.5 us
    ppermute x2, starting transfers between devices, extended(): lax.ppermute(tail, axis, [(i, (i + 1) % count) for i in range(ends)])  6.25 us
  transfers between devices with their start and end apart: 5, of which 3 were waited for; matrix products, arithmetic and copies ran while one was open for 0% of the time, Pallas kernels for 0%

commit v1 on v0

--- a/solution.py
+++ b/solution.py
@@ -55,7 +55,9 @@
     oxid_next = oxidizer + 0.15 * (diffuse_local(widened[1], widened[2]) + react)
     rows = 2 * fuel.shape[0] * fuel.shape[1] * lax.axis_size("gx") * lax.axis_size("gy")
     gram = local_gram(fuel_next, oxid_next) / rows
-    total = lax.psum(gram, ("gx", "gy"))
+    total = gram
+    for b in ("gy", "gx"):
+        total = lax.psum(total, b)
     factor = jnp.linalg.cholesky(total).T
     return (fuel_next, oxid_next, factor)
 

time: 273 us -> 255 us (0.934)
  waiting for transfers between devices: 172 us -> 154 us
    psum x1 -> x2, waiting for transfers between devices: 132 us -> 114 us  [shards(): total = lax.psum(total, b)]
  transfers between devices with their start and end apart: 5 -> 6, of which waited for: 3 -> 4; matrix products, arithmetic and copies ran while one was open for 0% -> 0% of each run, Pallas kernels for 0% -> 0%
where the time goes in v1:
time: 255 us
  waiting for transfers between devices  154 us (60%)
  other arithmetic  67.9 us (27%)
  between operations  16.1 us (6%)
  starting transfers between devices  9.09 us (4%)
  matrix products  4.54 us (2%)
  local copies, waits for them, and re-layouts  3.59 us (1%)
    psum x2, waiting for transfers between devices, shards(): total = lax.psum(total, b)  114 us
    another operation x10, other arithmetic, shards(): factor = jnp.linalg.cholesky(total).T  56.4 us
    ppermute x2, waiting for transfers between devices, extended(): lax.ppermute(tail, axis, [(i, (i + 1) % count) for i in range(ends)])  36.5 us
    ppermute x2, starting transfers between devices, extended(): lax.ppermute(tail, axis, [(i, (i + 1) % count) for i in range(ends)])  6.25 us
  transfers between devices with their start and end apart: 6, of which 4 were waited for; matrix products, arithmetic and copies ran while one was open for 0% of the time, Pallas kernels for 0%

profile of v1, /device:TPU:0, one launch (start us, length us, event | category | flops | bytes accessed | tf_op | source)
XLA Modules:
  0.0 254.9 jit_solution(8324672264682265762)
XLA Ops:
  7.2 0.0 copy-start.1
  7.2 0.0 copy-start
  7.2 0.0 copy-start.2
  7.2 0.0 all-reduce.5.cloned.1.call-start
  7.2 1.7 pad_maximum_fusion
  8.9 0.1 fusion.45
  9.0 5.0 %collective-permute-start = (f32[3,1,192,384]{3,2,1,0:T(8,128)S(1)}, f32[3,1,192,384]{3,2,1,0:T(8,128)S(1)}, u32[]{:S(2)}, u32[]{:S(2)}) collective-permute-start(f32[3,1,192,384]{3,2,1,0:T(8,128)S(1)} %get-tuple-element.11), channel_id=1, source_target_pairs={{0,4},{4,8},{8,12},{12,16},{16,20},{20,24},{24,28},{1,5},{5,9},{9,... | collective-permute-start | bytes 2654216 | tf_op jit(solution)/shard_map/ppermute | solution.py:15
  14.0 1.3 collective-permute-start.1
  15.3 36.5 %collective-permute-done = f32[3,1,192,384]{3,2,1,0:T(8,128)S(1)} collective-permute-done((f32[3,1,192,384]{3,2,1,0:T(8,128)S(1)}, f32[3,1,192,384]{3,2,1,0:T(8,128)S(1)}, u32[]{:S(2)}, u32[]{:S(2)}) %collective-permute-start) | collective-permute-done | bytes 884768 | tf_op jit(solution)/shard_map/ppermute | solution.py:15
  51.8 0.0 collective-permute-done.1
  51.8 0.0 copy-done.1
  51.8 0.0 copy-done
  51.8 0.0 copy-done.2
  51.8 1.3 collective-permute-start.2
  53.1 1.3 collective-permute-start.3
  54.4 0.0 collective-permute-done.2
  54.4 3.5 %collective-permute-done.3 = f32[3,4,1,384]{3,2,1,0:T(1,128)S(1)} collective-permute-done((f32[3,4,1,384]{3,2,1,0:T(1,128)S(1)}, f32[3,4,1,384]{3,2,1,0:T(1,128)S(1)}, u32[]{:S(2)}, u32[]{:S(2)}) %collective-permute-start.3) | collective-permute-done | bytes 18464 | tf_op jit(solution)/shard_map/ppermute | solution.py:17
  57.9 4.6 %select_maximum_fusion = f32[3,4,194,386]{3,2,1,0:T(8,128)S(1)} fusion(f32[3,4,1,384]{3,2,1,0:T(1,128)S(1)} %collective-permute-done.3, f32[3,4,1,384]{3,2,1,0:T(1,128)S(1)} %collective-permute-done.2, f32[3,1,192,384]{3,2,1,0:T(8,128)S(1)} %collective-permute-done.1, f32[3,1,192,384]{3,2,1,0:T(8,128)S(1)} %collective-permute-done, ...), kind=kLoop, calls=%fused_computation.2 | loop fusion | flops 14377728 | bytes 7170240 | tf_op jit(solution)/shard_map/concatenate | solution.py:13
  62.5 0.0 copy-start.5
  62.5 0.5 slice_bitcast_fusion
  63.1 0.5 copy-done.5
  63.6 2.0 fusion.7
  65.6 0.0 copy-start.3
  65.7 2.0 fusion.21
  67.7 0.0 copy-done.3
  67.7 0.0 copy-start.4
  67.7 1.4 convolution_bitcast_fusion
  69.1 2.1 fusion.2
  71.3 0.0 all-reduce.5.cloned.1.call-update
  71.3 0.2 all-reduce.7.cloned.1.call-start
  71.5 37.0 %all-reduce.5.cloned.1.call-done = f32[384,384]{0,1:T(8,128)} async-done(((f32[384,384]{0,1:T(8,128)}), f32[384,384]{0,1:T(8,128)}) %all-reduce.5.cloned.1.call-update) | async-done | bytes 589840 | tf_op jit(solution)/shard_map/psum | solution.py:60
  108.6 0.0 all-reduce.7.cloned.1.call-update
  108.6 76.6 %all-reduce.7.cloned.1.call-done = f32[384,384]{0,1:T(8,128)} async-done(((f32[384,384]{0,1:T(8,128)}), f32[384,384]{0,1:T(8,128)}) %all-reduce.7.cloned.1.call-update) | async-done | bytes 589840 | tf_op jit(solution)/shard_map/psum | solution.py:60
  185.2 1.3 copy.9
  186.5 1.1 fusion.37
  187.6 11.7 %cholesky.77 = f32[128,128]{1,0:T(8,128)S(1)} custom-call(f32[128,128]{1,0:T(8,128)S(1)} %cholesky.192), custom_call_target="Cholesky" | custom-call | tf_op jit(solution)/shard_map/jit(cholesky)/cholesky | solution.py:61
  199.4 9.8 %custom-call.19 = f32[1,128,128]{1,2,0:T(8,128)S(1)} custom-call(f32[1,128,128]{2,1,0:T(8,128)S(1)} %get-tuple-element.19), custom_call_target="InvertDiagBlocksLowerTriangular" | custom-call | tf_op jit(solution)/shard_map/jit(cholesky)/cholesky | solution.py:61
  209.2 0.3 constant_dynamic-update-slice_fusion.1
  209.5 0.3 convolution_subtract_fusion
  209.8 0.0 copy-done.4
  209.8 11.7 %cholesky.162 = f32[128,128]{1,0:T(8,128)S(1)} custom-call(f32[128,128]{1,0:T(8,128)S(1)} %cholesky.196), custom_call_target="Cholesky" | custom-call | tf_op jit(solution)/shard_map/jit(cholesky)/cholesky | solution.py:61
  221.6 10.0 %custom-call.20 = f32[1,128,128]{1,2,0:T(8,128)S(1)} custom-call(f32[1,128,128]{2,1,0:T(8,128)S(1)} %get-tuple-element.16), custom_call_target="InvertDiagBlocksLowerTriangular" | custom-call | tf_op jit(solution)/shard_map/jit(cholesky)/cholesky | solution.py:61
  231.6 0.2 convolution_dynamic-update-slice_fusion
  231.8 0.3 convolution_subtract_fusion.1
  232.1 11.7 %cholesky.181 = f32[128,128]{1,0:T(8,128)S(1)} custom-call(f32[128,128]{1,0:T(8,128)S(1)} %convolution_subtract_fusion.1), custom_call_target="Cholesky" | custom-call | tf_op jit(solution)/shard_map/jit(cholesky)/cholesky | solution.py:61
  243.8 0.6 compare_reduce_fusion
  244.4 0.7 compare_reduce_fusion.1
  247.0 1.1 copy.10
  (8 shorter events, 0.2 us)
Async XLA Ops:
  7.2 44.6 %copy-start.1 = (f32[2,192,384]{2,1,0:T(8,128)S(1)}, f32[2,192,384]{2,1,0:T(8,128)}, u32[]{:S(2)}) copy-start(f32[2,192,384]{2,1,0:T(8,128)} %param.5) | copy-start | bytes 1769476
  7.2 44.6 %copy-start = (f32[2,192,384]{2,1,0:T(8,128)S(1)}, f32[2,192,384]{2,1,0:T(8,128)}, u32[]{:S(2)}) copy-start(f32[2,192,384]{2,1,0:T(8,128)} %param.4) | copy-start | bytes 1769476
  7.2 44.6 %copy-start.2 = (f32[2,192,384]{2,1,0:T(8,128)S(1)}, f32[2,192,384]{2,1,0:T(8,128)}, u32[]{:S(2)}) copy-start(f32[2,192,384]{2,1,0:T(8,128)} %param.6) | copy-start | bytes 1769476
  7.2 101.4 %all-reduce.5.cloned.1.call-start = ((), (), s32[]{:S(2)}) async-start(), calls=%async_computation | async-start | bytes 1179648 | tf_op jit(solution)/shard_map/psum | solution.py:60
  9.0 42.8 %collective-permute-start = (f32[3,1,192,384]{3,2,1,0:T(8,128)S(1)}, f32[3,1,192,384]{3,2,1,0:T(8,128)S(1)}, u32[]{:S(2)}, u32[]{:S(2)}) collective-permute-start(f32[3,1,192,384]{3,2,1,0:T(8,128)S(1)} %get-tuple-element.11), channel_id=1, source_target_pairs={{0,4},{4,8},{8,12},{12,16},{16,20},{20,24},{24,28},{1,5},{5,9},{9,... | collective-permute-start | bytes 2654216 | tf_op jit(solution)/shard_map/ppermute | solution.py:15
  14.0 37.8 %collective-permute-start.1 = (f32[3,1,192,384]{3,2,1,0:T(8,128)S(1)}, f32[3,1,192,384]{3,2,1,0:T(8,128)S(1)}, u32[]{:S(2)}, u32[]{:S(2)}) collective-permute-start(f32[3,1,192,384]{3,2,1,0:T(8,128)S(1)} %get-tuple-element.12), channel_id=1, source_target_pairs={{4,0},{8,4},{12,8},{16,12},{20,16},{24,20},{28,24},{5,1},{9,5},{13... | collective-permute-start | bytes 2654216 | tf_op jit(solution)/shard_map/ppermute | solution.py:17
  51.8 2.6 %collective-permute-start.2 = (f32[3,4,1,384]{3,2,1,0:T(1,128)S(1)}, f32[3,4,1,384]{3,2,1,0:T(1,128)S(1)}, u32[]{:S(2)}, u32[]{:S(2)}) collective-permute-start(f32[3,4,1,384]{3,2,1,0:T(1,128)S(1)} %get-tuple-element.9), channel_id=1, source_target_pairs={{0,1},{1,2},{2,3},{4,5},{5,6},{6,7},{8,9},{9,10},{10,11},{12,13},{... | collective-permute-start | bytes 55304 | tf_op jit(solution)/shard_map/ppermute | solution.py:15
  53.1 4.8 %collective-permute-start.3 = (f32[3,4,1,384]{3,2,1,0:T(1,128)S(1)}, f32[3,4,1,384]{3,2,1,0:T(1,128)S(1)}, u32[]{:S(2)}, u32[]{:S(2)}) collective-permute-start(f32[3,4,1,384]{3,2,1,0:T(1,128)S(1)} %get-tuple-element.10), channel_id=1, source_target_pairs={{1,0},{2,1},{3,2},{5,4},{6,5},{7,6},{9,8},{10,9},{11,10},{13,12},{... | collective-permute-start | bytes 55304 | tf_op jit(solution)/shard_map/ppermute | solution.py:17
  62.5 1.1 copy-start.5
  65.6 2.1 copy-start.3
  67.7 142.1 %copy-start.4 = (f32[2,192,384]{2,1,0:T(8,128)}, f32[2,192,384]{2,1,0:T(8,128)S(1)}, u32[]{:S(2)}) copy-start(f32[2,192,384]{2,1,0:T(8,128)S(1)} %fusion.21) | copy-start | bytes 1769476
  71.3 113.9 %all-reduce.7.cloned.1.call-start = ((), (), s32[]{:S(2)}) async-start(), calls=%async_computation.1 | async-start | bytes 1179648 | tf_op jit(solution)/shard_map/psum | solution.py:60
Sparse Core Ops, SparseCore 0:
  71.4 37.0 all-reduce.4
  111.9 73.2 all-reduce.6
